TPU v7x, 32 devices: a whole 2x2x4 slice. The times are simulated.
32 devices in a mesh: tm: 4 (over y, core), space: 8 (over z, x).
Axes of the slice: x: 2, y: 2, z: 4, core: 2. Of those that a mesh axis runs over, the one named last changes fastest.
Arguments:
- patches: bfloat16 [16, 128, 512], P('tm', 'space'), may hold values from -6 to 6
- owner_list: int32 [128], replicated, may hold values from 0 to 7, as said below
- valid_rows: int32 [128], replicated, may hold values from 1 to 8, as said below
- embed_weight: bfloat16 [64, 3072], replicated, may hold values from -0.75 to 0.75
- embed_bias: float32 [3072], replicated, may hold values from -3 to 3
- norm_gain: float32 [4, 3072], replicated, may hold values from 0.5 to 1.5
- conv_kernel: float32 [4, 3, 3072], replicated, may hold values from -3 to 3
- conv_bias: float32 [4, 3072], replicated, may hold values from -3 to 3
Outputs:
- packed: bfloat16 [16, 256, 8, 3072], P('tm', 'space')
Inputs may be any that keep to these rules, and one draw needn't show every extreme that they name: `owner_list`: among the tiles of one source device (tiles s * 16 to (s + 1) * 16 - 1) no owner appears more than 4 times; some owner appears exactly 4 times among the tiles of every source device, so it receives 2 * 16 tiles. `valid_rows`: some tile has all 8 rows live.
All inputs are finite; a program needn't handle non-finite values.
Results may differ from a plain program's by a relative error of at most 0.009.
Values may be sent and summed in bfloat16 or wider, within the bound.
No kernel may reach another device: no remote copies, remote signals or barrier semaphores. Data moves between devices by JAX's collectives and lax.ppermute only.
A program may use at most 64 MiB of HBM per device.

v0:
```python
import jax
import jax.numpy as jnp
from jax import lax
from jax.sharding import PartitionSpec as P

D = 3072
PF = 64
LAYERS = 4
F_DEV = 4
TILES_DEV = 16
TILE_ROWS = 8


def from_behind(value, axis, by):
    devices = lax.axis_size(axis)
    pairs = [(i, i + by) for i in range(devices) if 0 <= i + by < devices]
    return lax.ppermute(value, axis, pairs)


def rms_scale(values, gain_row):
    mean_square = jnp.mean(values * values, axis=-1, keepdims=True)
    return values * lax.rsqrt(mean_square + 1e-06) * gain_row


def per_device(
    patches, owner_list, valid_rows, embed_weight, embed_bias, norm_gain, conv_kernel, conv_bias
):
    sources = lax.axis_size("space")
    per_pair = 2 * TILES_DEV // sources
    slot_count = sources * per_pair
    my_index = lax.axis_index("space")
    owner_grid = owner_list.reshape(sources, TILES_DEV)
    same_owner = owner_grid[:, :, None] == owner_grid[:, None, :]
    earlier = jnp.arange(TILES_DEV)[None, :] < jnp.arange(TILES_DEV)[:, None]
    order_in = jnp.sum((same_owner & earlier[None]).astype(jnp.int32), axis=-1)
    source_ids = jnp.arange(sources, dtype=jnp.int32)[:, None]
    slot_of = (owner_grid * slot_count + source_ids * per_pair + order_in).reshape(-1)
    send_place = lax.dynamic_index_in_dim(
        owner_grid * per_pair + order_in, my_index, 0, keepdims=False
    )
    matches = jnp.arange(slot_count, dtype=jnp.int32)[:, None] == send_place[None, :]
    chosen_tiles = jnp.sum(
        jnp.where(matches, jnp.arange(TILES_DEV, dtype=jnp.int32)[None, :], 0), axis=1
    )
    received = (
        slot_of[None, :] == my_index * slot_count + jnp.arange(slot_count, dtype=jnp.int32)[:, None]
    )
    slot_rows = jnp.sum(jnp.where(received, valid_rows[None, :], 0), axis=1)
    live_rows = jnp.arange(TILE_ROWS, dtype=jnp.int32)[None, :] < slot_rows[:, None]
    frame_count = patches.shape[0]
    tile_count = patches.shape[1]
    flat_rows = patches.reshape(frame_count * tile_count * TILE_ROWS, PF)
    hidden = jnp.dot(flat_rows, embed_weight, preferred_element_type=jnp.float32) + embed_bias
    hidden = hidden.astype(jnp.bfloat16).reshape(frame_count, tile_count, TILE_ROWS, D)
    for layer in range(LAYERS):
        earlier_frames = from_behind(hidden[F_DEV - 2 :], "tm", 1)
        framed = jnp.concatenate([earlier_frames, hidden], axis=0)
        normed = rms_scale(framed.astype(jnp.float32), norm_gain[layer])
        mixed = (
            conv_kernel[layer, 0] * normed[2:]
            + conv_kernel[layer, 1] * normed[1:-1]
            + conv_kernel[layer, 2] * normed[:-2]
            + conv_bias[layer]
        )
        hidden = (framed[2:].astype(jnp.float32) + jax.nn.silu(mixed)).astype(jnp.bfloat16)
    outgoing = jnp.take(hidden, chosen_tiles, axis=1)
    arrived = lax.all_to_all(outgoing, "space", split_axis=1, concat_axis=1, tiled=True)
    return jnp.where(live_rows[None, :, :, None], arrived, jnp.zeros_like(arrived))


def solution(mesh):
    placed = (P("tm", "space", None), P(), P(), P(), P(), P(), P(), P())
    return jax.shard_map(
        per_device,
        mesh=mesh,
        in_specs=placed,
        out_specs=P("tm", "space", None, None),
        check_vma=False,
    )
```

profile of v0, /device:TPU:9, one launch (start us, length us, event | category | flops | bytes accessed | tf_op | source)
XLA Modules:
  0.0 274.9 jit_solution(15942792516109363353)
XLA Ops:
  0.0 0.0 copy-start
  0.0 1.7 reshape.136
  1.7 1.9 add_convert_fusion.4
  3.6 0.1 slice.150
  3.7 3.7 %collective-permute-start = (bf16[2,16,8,3072]{3,2,1,0:T(8,128)(2,1)S(1)}, bf16[2,16,8,3072]{3,2,1,0:T(8,128)(2,1)S(1)}, u32[]{:S(2)}, u32[]{:S(2)}) collective-permute-start(bf16[2,16,8,3072]{3,2,1,0:T(8,128)(2,1)S(1)} %bitcast.37), channel_id=1, source_target_pairs={{0,8},{8,16},{16,24},{1,9},{9,17},{17,25},{2,10},{10,18},{18,26},{... | collective-permute-start | bytes 4718600 | tf_op jit(solution)/shard_map/ppermute | solution.py:17
  7.4 0.6 fusion.23
  8.1 0.6 fusion.22
  8.7 0.7 fusion.21
  9.4 15.4 %collective-permute-done = bf16[2,16,8,3072]{3,2,1,0:T(8,128)(2,1)S(1)} collective-permute-done((bf16[2,16,8,3072]{3,2,1,0:T(8,128)(2,1)S(1)}, bf16[2,16,8,3072]{3,2,1,0:T(8,128)(2,1)S(1)}, u32[]{:S(2)}, u32[]{:S(2)}) %collective-permute-start) | collective-permute-done | bytes 1572896 | tf_op jit(solution)/shard_map/ppermute | solution.py:17
  24.8 1.0 fusion
  25.8 1.6 fusion.1
  27.4 3.2 %add_convert_fusion.3 = bf16[4,16,8,3072]{3,2,1,0:T(8,128)(2,1)S(1)} fusion(f32[6,16,8,3072]{3,2,1,0:T(8,128)S(1)} %fusion.1, f32[3072]{0:T(1024)S(1)} %bitcast.44, f32[3072]{0:T(1024)S(1)} %bitcast.38, f32[3072]{0:T(1024)S(1)} %bitcast.40, f32[3072]{0:T(1024)S(1)} %bitcast.42, bf16[512,3072]{1,0:T(8,128)(2,1)S(1)} %add_convert_fusion.4), kind=kLoop, calls=%fused_computation.45 | loop fusion | flops 20447232 | bytes 25214976 | tf_op jit(solution)/shard_map/convert_element_type | solution.py:65
  30.6 0.0 copy-start.5
  30.6 0.1 slice.154
  30.7 4.4 %collective-permute-start.1 = (bf16[2,16,8,3072]{3,2,1,0:T(8,128)(2,1)S(1)}, bf16[2,16,8,3072]{3,2,1,0:T(8,128)(2,1)S(1)}, u32[]{:S(2)}, u32[]{:S(2)}) collective-permute-start(bf16[2,16,8,3072]{3,2,1,0:T(8,128)(2,1)S(1)} %slice.154), channel_id=1, source_target_pairs={{0,8},{8,16},{16,24},{1,9},{9,17},{17,25},{2,10},{10,18},{18,26},{... | collective-permute-start | bytes 4718600 | tf_op jit(solution)/shard_map/ppermute | solution.py:17
  35.1 17.3 %collective-permute-done.1 = bf16[2,16,8,3072]{3,2,1,0:T(8,128)(2,1)S(1)} collective-permute-done((bf16[2,16,8,3072]{3,2,1,0:T(8,128)(2,1)S(1)}, bf16[2,16,8,3072]{3,2,1,0:T(8,128)(2,1)S(1)}, u32[]{:S(2)}, u32[]{:S(2)}) %collective-permute-start.1) | collective-permute-done | bytes 1572896 | tf_op jit(solution)/shard_map/ppermute | solution.py:17
  52.5 1.0 fusion.2
  53.5 2.9 %fusion.3 = f32[6,16,8,3072]{3,2,1,0:T(8,128)S(1)} fusion(f32[3072]{0:T(1024)S(1)} %bitcast.60, f32[6,16,8]{2,1,0:T(8,128)S(1)} %add_rsqrt_fusion.2, bf16[4,16,8,3072]{3,2,1,0:T(8,128)(2,1)} %copy-done.5, bf16[2,16,8,3072]{3,2,1,0:T(8,128)(2,1)S(1)} %collective-permute-done.1), kind=kLoop, calls=%fused_computation.12 | loop fusion | flops 9437184 | bytes 14171136 | tf_op jit(solution)/shard_map/mul | solution.py:22
  56.4 6.7 %add_convert_fusion.2 = bf16[4,16,8,3072]{3,2,1,0:T(8,128)(2,1)} fusion(f32[6,16,8,3072]{3,2,1,0:T(8,128)S(1)} %fusion.3, f32[3072]{0:T(1024)S(1)} %bitcast.49, f32[3072]{0:T(1024)S(1)} %bitcast.46, f32[3072]{0:T(1024)S(1)} %bitcast.47, f32[3072]{0:T(1024)S(1)} %bitcast.48, f32[3072]{0:T(1024)S(1)} %bitcast.45, f32[6,16,8,3072]{3,2,1,0:T(8,128)S(1)} %fusion.1, ...), kind=kLoop, calls=%fused_computation.44 | loop fusion | flops 40894464 | bytes 44138496 | tf_op jit(solution)/shard_map/convert_element_type | solution.py:65
  63.1 1.7 slice.158
  64.8 4.6 %collective-permute-start.2 = (bf16[2,16,8,3072]{3,2,1,0:T(8,128)(2,1)S(1)}, bf16[2,16,8,3072]{3,2,1,0:T(8,128)(2,1)S(1)}, u32[]{:S(2)}, u32[]{:S(2)}) collective-permute-start(bf16[2,16,8,3072]{3,2,1,0:T(8,128)(2,1)S(1)} %slice.158), channel_id=1, source_target_pairs={{0,8},{8,16},{16,24},{1,9},{9,17},{17,25},{2,10},{10,18},{18,26},{... | collective-permute-start | bytes 4718600 | tf_op jit(solution)/shard_map/ppermute | solution.py:17
  69.4 17.2 %collective-permute-done.2 = bf16[2,16,8,3072]{3,2,1,0:T(8,128)(2,1)S(1)} collective-permute-done((bf16[2,16,8,3072]{3,2,1,0:T(8,128)(2,1)S(1)}, bf16[2,16,8,3072]{3,2,1,0:T(8,128)(2,1)S(1)}, u32[]{:S(2)}, u32[]{:S(2)}) %collective-permute-start.2) | collective-permute-done | bytes 1572896 | tf_op jit(solution)/shard_map/ppermute | solution.py:17
  86.5 2.9 %fusion.4 = f32[6,16,8]{2,1,0:T(8,128)S(1)} fusion(bf16[4,16,8,3072]{3,2,1,0:T(8,128)(2,1)} %add_convert_fusion.2, bf16[2,16,8,3072]{3,2,1,0:T(8,128)(2,1)S(1)} %collective-permute-done.2), kind=kLoop, calls=%fused_computation.13 | loop fusion | flops 9436416 | bytes 4721664 | tf_op jit(solution)/shard_map/reduce_sum | solution.py:21
  89.5 1.6 fusion.5
  91.1 0.0 copy-start.13
  91.1 3.2 %add_convert_fusion.1 = bf16[4,16,8,3072]{3,2,1,0:T(8,128)(2,1)S(1)} fusion(f32[6,16,8,3072]{3,2,1,0:T(8,128)S(1)} %fusion.5, bf16[4,16,8,3072]{3,2,1,0:T(8,128)(2,1)S(1)} %copy-done.2, f32[3072]{0:T(1024)S(1)} %bitcast.59, f32[3072]{0:T(1024)S(1)} %bitcast.53, f32[3072]{0:T(1024)S(1)} %bitcast.54, f32[3072]{0:T(1024)S(1)} %bitcast.55), kind=kLoop, calls=%fused_computation.43 | loop fusion | flops 20447232 | bytes 25214976 | tf_op jit(solution)/shard_map/convert_element_type | solution.py:65
  94.3 0.0 copy-start.3
  94.3 1.7 copy-done.3
  95.9 1.3 slice.162
  97.2 4.6 %collective-permute-start.3 = (bf16[2,16,8,3072]{3,2,1,0:T(8,128)(2,1)}, bf16[2,16,8,3072]{3,2,1,0:T(8,128)(2,1)}, u32[]{:S(2)}, u32[]{:S(2)}) collective-permute-start(bf16[2,16,8,3072]{3,2,1,0:T(8,128)(2,1)} %slice.162), channel_id=1, source_target_pairs={{0,8},{8,16},{16,24},{1,9},{9,17},{17,25},{2,10},{10,18},{18,26},{... | collective-permute-start | bytes 4718600 | tf_op jit(solution)/shard_map/ppermute | solution.py:17
  101.9 0.1 eq.43
  101.9 0.3 convert_reduce_fusion
  102.3 0.1 select_reduce_fusion.1
  102.4 17.1 %collective-permute-done.3 = bf16[2,16,8,3072]{3,2,1,0:T(8,128)(2,1)} collective-permute-done((bf16[2,16,8,3072]{3,2,1,0:T(8,128)(2,1)}, bf16[2,16,8,3072]{3,2,1,0:T(8,128)(2,1)}, u32[]{:S(2)}, u32[]{:S(2)}) %collective-permute-start.3) | collective-permute-done | bytes 1572896 | tf_op jit(solution)/shard_map/ppermute | solution.py:17
  119.5 3.4 %fusion.6 = f32[6,16,8]{2,1,0:T(8,128)S(1)} fusion(bf16[4,16,8,3072]{3,2,1,0:T(8,128)(2,1)} %copy-done.3, bf16[2,16,8,3072]{3,2,1,0:T(8,128)(2,1)} %collective-permute-done.3), kind=kLoop, calls=%fused_computation.15 | loop fusion | flops 9436416 | bytes 4721664 | tf_op jit(solution)/shard_map/reduce_sum | solution.py:21
  122.9 2.7 fusion.7
  125.6 4.3 %add_convert_fusion = bf16[4,16,8,3072]{3,2,1,0:T(8,128)(2,1)} fusion(f32[6,16,8,3072]{3,2,1,0:T(8,128)S(1)} %fusion.7, bf16[4,16,8,3072]{3,2,1,0:T(8,128)(2,1)S(1)} %copy-done.4, f32[3072]{0:T(1024)S(1)} %bitcast.56, f32[3072]{0:T(1024)S(1)} %bitcast.51, f32[3072]{0:T(1024)S(1)} %bitcast.52, f32[3072]{0:T(1024)S(1)} %bitcast.50), kind=kLoop, calls=%fused_computation.42 | loop fusion | flops 20447232 | bytes 25214976 | tf_op jit(solution)/shard_map/convert_element_type | solution.py:65
  130.0 5.5 %gather_fusion = bf16[32,4,8,3072]{3,2,1,0:T(8,128)(2,1)} fusion(bf16[4,16,8,3072]{3,2,1,0:T(8,128)(2,1)} %add_convert_fusion, s32[1024]{0:T(1024)S(1)} %pad_clamp_fusion), kind=kCustom, calls=%fused_computation | custom fusion | bytes 12583040 | tf_op jit(solution)/shard_map/jit(_take)/gather | solution.py:66
  135.5 6.2 %select_bitcast_fusion = bf16[4,32,8,3072]{3,2,0,1:T(8,128)(2,1)} fusion(bf16[32,4,8,3072]{3,2,1,0:T(8,128)(2,1)} %gather_fusion, pred[32]{0:T(512)(128)(4,1)S(1)} %compare_and_fusion), kind=kLoop, calls=%fused_computation.41 | loop fusion | flops 3145728 | bytes 12582944 | tf_op jit(solution)/shard_map/jit(_take)/select_n | solution.py:66
  141.7 5.8 %all-to-all-start = ((bf16[4,32,8,3072]{3,2,0,1:T(8,128)(2,1)}), bf16[4,32,8,3072]{3,2,0,1:T(8,128)(2,1)}, u32[]{:S(2)}, u32[]{:S(2)}) async-start(bf16[4,32,8,3072]{3,2,0,1:T(8,128)(2,1)} %select_bitcast_fusion), calls=%async_computation | async-start | bytes 12582912 | tf_op jit(solution)/shard_map/all_to_all | solution.py:67
  147.5 0.1 reduce_sum.68
  147.6 0.1 add.185
  147.7 0.1 add.186
  147.8 0.2 select_reduce_fusion
  147.9 0.1 iota_compare_fusion
  148.0 120.5 %all-to-all-done = bf16[4,32,8,3072]{3,2,0,1:T(8,128)(2,1)} async-done(((bf16[4,32,8,3072]{3,2,0,1:T(8,128)(2,1)}), bf16[4,32,8,3072]{3,2,0,1:T(8,128)(2,1)}, u32[]{:S(2)}, u32[]{:S(2)}) %all-to-all-start) | async-done | bytes 6291488 | tf_op jit(solution)/shard_map/all_to_all | solution.py:67
  268.5 3.3 %broadcast_select_fusion = bf16[4,32,8,3072]{3,2,0,1:T(8,128)(2,1)S(1)} fusion(bf16[4,32,8,3072]{3,2,0,1:T(8,128)(2,1)} %all-to-all-done, pred[32,8]{1,0:T(8,128)(4,1)S(1)} %iota_compare_fusion), kind=kLoop, calls=%fused_computation.47 | loop fusion | flops 3145728 | bytes 12583168 | tf_op jit(solution)/shard_map/jit(_where)/select_n | solution.py:68
  271.8 3.1 %copy.10 = bf16[4,32,8,3072]{3,2,1,0:T(8,128)(2,1)} copy(bf16[4,32,8,3072]{3,2,0,1:T(8,128)(2,1)S(1)} %broadcast_select_fusion) | data formatting | bytes 12582912 | tf_op jit(solution)/shard_map/jit(_where)/select_n | solution.py:68
  (38 shorter events, 0.2 us)
Async XLA Ops:
  0.0 1.7 copy-start
  1.7 5.7 %copy-start.11 = (f32[4,3072]{1,0:T(4,128)S(1)}, f32[4,3072]{1,0:T(4,128)}, u32[]{:S(2)}) copy-start(f32[4,3072]{1,0:T(4,128)} %param.13) | copy-start | bytes 147460
  1.7 6.4 %copy-start.12 = (f32[4,3072]{1,0:T(4,128)S(1)}, f32[4,3072]{1,0:T(4,128)}, u32[]{:S(2)}) copy-start(f32[4,3072]{1,0:T(4,128)} %param.15) | copy-start | bytes 147460
  1.7 7.0 %copy-start.6 = (f32[4,3,3072]{2,0,1:T(4,128)S(1)}, f32[4,3,3072]{2,0,1:T(4,128)}, u32[]{:S(2)}) copy-start(f32[4,3,3072]{2,0,1:T(4,128)} %param.14) | copy-start | bytes 442372
  3.7 21.1 %collective-permute-start = (bf16[2,16,8,3072]{3,2,1,0:T(8,128)(2,1)S(1)}, bf16[2,16,8,3072]{3,2,1,0:T(8,128)(2,1)S(1)}, u32[]{:S(2)}, u32[]{:S(2)}) collective-permute-start(bf16[2,16,8,3072]{3,2,1,0:T(8,128)(2,1)S(1)} %bitcast.37), channel_id=1, source_target_pairs={{0,8},{8,16},{16,24},{1,9},{9,17},{17,25},{2,10},{10,18},{18,26},{... | collective-permute-start | bytes 4718600 | tf_op jit(solution)/shard_map/ppermute | solution.py:17
  30.6 22.9 %copy-start.5 = (bf16[4,16,8,3072]{3,2,1,0:T(8,128)(2,1)}, bf16[4,16,8,3072]{3,2,1,0:T(8,128)(2,1)S(1)}, u32[]{:S(2)}) copy-start(bf16[4,16,8,3072]{3,2,1,0:T(8,128)(2,1)S(1)} %add_convert_fusion.3) | copy-start | bytes 9437188
  30.7 21.7 %collective-permute-start.1 = (bf16[2,16,8,3072]{3,2,1,0:T(8,128)(2,1)S(1)}, bf16[2,16,8,3072]{3,2,1,0:T(8,128)(2,1)S(1)}, u32[]{:S(2)}, u32[]{:S(2)}) collective-permute-start(bf16[2,16,8,3072]{3,2,1,0:T(8,128)(2,1)S(1)} %slice.154), channel_id=1, source_target_pairs={{0,8},{8,16},{16,24},{1,9},{9,17},{17,25},{2,10},{10,18},{18,26},{... | collective-permute-start | bytes 4718600 | tf_op jit(solution)/shard_map/ppermute | solution.py:17
  63.1 26.3 %copy-start.2 = (bf16[4,16,8,3072]{3,2,1,0:T(8,128)(2,1)S(1)}, bf16[4,16,8,3072]{3,2,1,0:T(8,128)(2,1)}, u32[]{:S(2)}) copy-start(bf16[4,16,8,3072]{3,2,1,0:T(8,128)(2,1)} %add_convert_fusion.2) | copy-start | bytes 9437188
  64.8 21.7 %collective-permute-start.2 = (bf16[2,16,8,3072]{3,2,1,0:T(8,128)(2,1)S(1)}, bf16[2,16,8,3072]{3,2,1,0:T(8,128)(2,1)S(1)}, u32[]{:S(2)}, u32[]{:S(2)}) collective-permute-start(bf16[2,16,8,3072]{3,2,1,0:T(8,128)(2,1)S(1)} %slice.158), channel_id=1, source_target_pairs={{0,8},{8,16},{16,24},{1,9},{9,17},{17,25},{2,10},{10,18},{18,26},{... | collective-permute-start | bytes 4718600 | tf_op jit(solution)/shard_map/ppermute | solution.py:17
  91.1 10.8 %copy-start.13 = (s32[128]{0:T(128)S(1)}, s32[128]{0:T(128)}, u32[]{:S(2)}) copy-start(s32[128]{0:T(128)} %param.9) | copy-start | bytes 1540
  94.3 1.7 copy-start.3
  95.9 26.9 %copy-start.10 = (f32[1,3072]{1,0:T(1,128)S(1)}, f32[1,3072]{1,0:T(1,128)}, u32[]{:S(2)}) copy-start(f32[1,3072]{1,0:T(1,128)} %get-tuple-element.23) | copy-start | bytes 36868
  97.2 25.7 %copy-start.4 = (bf16[4,16,8,3072]{3,2,1,0:T(8,128)(2,1)S(1)}, bf16[4,16,8,3072]{3,2,1,0:T(8,128)(2,1)}, u32[]{:S(2)}) copy-start(bf16[4,16,8,3072]{3,2,1,0:T(8,128)(2,1)} %copy-done.3) | copy-start | bytes 9437188
  97.2 22.3 %collective-permute-start.3 = (bf16[2,16,8,3072]{3,2,1,0:T(8,128)(2,1)}, bf16[2,16,8,3072]{3,2,1,0:T(8,128)(2,1)}, u32[]{:S(2)}, u32[]{:S(2)}) collective-permute-start(bf16[2,16,8,3072]{3,2,1,0:T(8,128)(2,1)} %slice.162), channel_id=1, source_target_pairs={{0,8},{8,16},{16,24},{1,9},{9,17},{17,25},{2,10},{10,18},{18,26},{... | collective-permute-start | bytes 4718600 | tf_op jit(solution)/shard_map/ppermute | solution.py:17
  122.9 2.7 copy-start.7
  122.9 2.7 copy-start.8
  122.9 2.7 copy-start.9
  141.7 6.1 %copy-start.14 = (s32[128]{0:T(128)S(1)}, s32[128]{0:T(128)}, u32[]{:S(2)}) copy-start(s32[128]{0:T(128)} %param.10) | copy-start | bytes 1540
  141.7 126.8 %all-to-all-start = ((bf16[4,32,8,3072]{3,2,0,1:T(8,128)(2,1)}), bf16[4,32,8,3072]{3,2,0,1:T(8,128)(2,1)}, u32[]{:S(2)}, u32[]{:S(2)}) async-start(bf16[4,32,8,3072]{3,2,0,1:T(8,128)(2,1)} %select_bitcast_fusion), calls=%async_computation | async-start | bytes 12582912 | tf_op jit(solution)/shard_map/all_to_all | solution.py:67
  268.5 6.5 %copy-start.1 = (bf16[64,3072]{1,0:T(8,128)(2,1)S(1)}, bf16[64,3072]{1,0:T(8,128)(2,1)}, u32[]{:S(2)}) copy-start(bf16[64,3072]{1,0:T(8,128)(2,1)} %param.11) | copy-start | bytes 1179652
where the time goes:
time: 279 us; the launch traced here: 275 us
  waiting for transfers between devices  187 us (67%)
  other arithmetic  44.7 us (16%)
  starting transfers between devices  23.1 us (8%)
  local copies, waits for them, and re-layouts  17.5 us (6%)
    all_to_all x1, waiting for transfers between devices, per_device(): lax.all_to_all(outgoing, 'space', split_axis=1, concat_axis=1, tiled=True)  120 us
    ppermute x4, waiting for transfers between devices, from_behind(): return lax.ppermute(value, axis, pairs)  67 us
    convert_element_type x4, other arithmetic, per_device(): (framed[2:].astype(jnp.float32) + jax.nn.silu(mixed)).astype(jnp.bfloat16)  17.4 us
    ppermute x4, starting transfers between devices, from_behind(): return lax.ppermute(value, axis, pairs)  17.3 us
    mul x4, other arithmetic, rms_scale(): return values * lax.rsqrt(mean_square + 1e-06) * gain_row  8.86 us
    reduce_sum x4, other arithmetic, rms_scale(): mean_square = jnp.mean(values * values, axis=-1, keepdims=True)  8.22 us
    select_n x2, other arithmetic, per_device(): outgoing = jnp.take(hidden, chosen_tiles, axis=1)  6.16 us
    all_to_all x1, starting transfers between devices, per_device(): lax.all_to_all(outgoing, 'space', split_axis=1, concat_axis=1, tiled=True)  5.82 us
  transfers between devices with their start and end apart: 5, of which 5 were waited for; matrix products, arithmetic and copies ran while one was open for 1% of the time, Pallas kernels for 0%

commit v1 on v0

v1 whole, which is shorter than its diff:
```python
import functools

import jax
import jax.numpy as jnp
from jax import lax
from jax.experimental import pallas as pl
from jax.experimental.pallas import tpu as pltpu
from jax.sharding import Mesh, PartitionSpec as P

D = 3072
PF = 64
LAYERS = 4
F_DEV = 4
TILES_DEV = 16
TILE_ROWS = 8
SLOTS_DEV = 2 * TILES_DEV
HALO = 2 * LAYERS
FRAMES_IN = HALO + F_DEV
LANES = 128
BLOCK = 16
MAX_ROWS = SLOTS_DEV * TILE_ROWS
COPIED = SLOTS_DEV * F_DEV


def send_kernel(sources, rows_out, me_ref, owner_ref, patches_ref, out_ref):
    per_pair = SLOTS_DEV // sources
    me = me_ref[0]
    lane = lax.broadcasted_iota(jnp.int32, (1, F_DEV * TILES_DEV), 1)
    tile = lane % TILES_DEV
    owners = [owner_ref[me * TILES_DEV + k] for k in range(TILES_DEV)]
    wanted = jnp.full((1, F_DEV * TILES_DEV), -1, jnp.int32)
    for k in range(TILES_DEV):
        order = jnp.int32(0)
        for before in range(k):
            order = order + (owners[before] == owners[k]).astype(jnp.int32)
        row = owners[k] * (F_DEV * per_pair) + order
        wanted = jnp.where(tile == k, row, wanted)
    wanted = wanted + (lane // TILES_DEV) * per_pair
    place = lax.broadcasted_iota(jnp.int32, (COPIED, F_DEV * TILES_DEV), 0)
    chosen = (place == wanted).astype(jnp.bfloat16)
    sent = jnp.dot(chosen, patches_ref[...], preferred_element_type=jnp.float32)
    sent = sent.astype(jnp.bfloat16)
    for copy in range(rows_out // COPIED):
        out_ref[copy * COPIED : (copy + 1) * COPIED, :] = sent


def main_kernel(
    sources,
    at_ref,
    owner_ref,
    valid_ref,
    got_ref,
    weight_ref,
    bias_ref,
    gain_ref,
    conv_ref,
    conv_bias_ref,
    out_ref,
    rows_ref,
    base_ref,
    place_ref,
    coef_ref,
    twice_ref,
    picked_ref,
    h_ref,
    square_ref,
    scale_ref,
    staged_ref,
    sems,
):
    per_pair = SLOTS_DEV // sources
    y, c, me = at_ref[0], at_ref[1], at_ref[2]
    frame0 = (2 * y + c) * F_DEV - HALO

    def clear(s, carry):
        rows_ref[s] = 0
        return carry

    lax.fori_loop(0, SLOTS_DEV, clear, 0)

    def one_source(s, carry):
        found = jnp.int32(0)
        for k in range(TILES_DEV):
            hit = owner_ref[s * TILES_DEV + k] == me
            where = jnp.where(hit, s * per_pair + found, SLOTS_DEV)
            rows_ref[where] = valid_ref[s * TILES_DEV + k]
            found = found + hit.astype(jnp.int32)
        return carry

    lax.fori_loop(0, sources, one_source, 0)

    row_in_tile = lax.broadcasted_iota(jnp.int32, (TILE_ROWS, LANES), 0)
    lane = lax.broadcasted_iota(jnp.int32, (1, LANES), 1)
    lane_slot = (lane // (F_DEV * per_pair)) * per_pair + lane % per_pair
    lane_frame = (lane % (F_DEV * per_pair)) // per_pair
    total = jnp.int32(0)
    first = jnp.full((1, LANES), 0, jnp.int32)
    after = jnp.full((1, LANES), 0, jnp.int32)
    for s in range(SLOTS_DEV):
        rows = rows_ref[s]
        base_ref[s] = total
        place_ref[s * TILE_ROWS : (s + 1) * TILE_ROWS, :] = jnp.where(
            row_in_tile < rows, total + row_in_tile, -1
        )
        first = jnp.where(lane_slot == s, total, first)
        total = total + rows
        after = jnp.where(lane_slot == s, total, after)
    blocks = (total + BLOCK - 1) // BLOCK

    for layer in range(LAYERS):
        gain = gain_ref[layer : layer + 1, :]
        for tap in range(3):
            row = 0.5 * conv_ref[layer * 3 + tap : layer * 3 + tap + 1, :] * gain
            coef_ref[layer, tap] = jnp.broadcast_to(row, (BLOCK, D)).astype(jnp.bfloat16)
        row = 0.5 * conv_bias_ref[layer : layer + 1, :]
        coef_ref[layer, 3] = jnp.broadcast_to(row, (BLOCK, D)).astype(jnp.bfloat16)
    twice_ref[:PF, :] = weight_ref[...]
    twice_ref[PF:, :] = weight_ref[...]

    behind = (jnp.maximum(y - 1, 0), c)
    before = (jnp.where(c == 1, y, jnp.maximum(y - 1, 0)), 1 - c)
    held = (behind, before, (y, c))

    def embed(b, carry):
        line = lax.broadcasted_iota(jnp.int32, (F_DEV * BLOCK, LANES), 0)
        row = line % BLOCK + b * BLOCK
        chosen = (row >= first) & (row < after) & (line // BLOCK == lane_frame)
        in_tile = jnp.sum(jnp.where(chosen, row - first, 0).astype(jnp.float32), axis=1, keepdims=True)
        chosen = chosen.astype(jnp.bfloat16)
        part = lax.broadcasted_iota(jnp.int32, (F_DEV * BLOCK, LANES), 1) // PF
        in_tile = in_tile.astype(jnp.int32)
        for d in range(3):
            yy, cc = held[d]
            wide = jnp.dot(chosen, got_ref[cc, yy], preferred_element_type=jnp.float32)
            own = jnp.zeros((F_DEV * BLOCK, LANES), jnp.float32)
            for q in range(TILE_ROWS * PF // LANES):
                own = jnp.where(part + 2 * q == in_tile, wide[:, q * LANES : (q + 1) * LANES], own)
            picked_ref[d * F_DEV * BLOCK : (d + 1) * F_DEV * BLOCK, :] = own.astype(jnp.bfloat16)
        rows = pl.ds(pl.multiple_of(b * BLOCK, BLOCK), BLOCK)
        squares = [None] * FRAMES_IN
        for n in range(D // 256):
            at = n * 256
            value = jnp.dot(
                picked_ref[...], twice_ref[:, at : at + 256], preferred_element_type=jnp.float32
            )
            value = (value + bias_ref[:, at : at + 256]).astype(jnp.bfloat16)
            for t in range(FRAMES_IN):
                piece = value[t * BLOCK : (t + 1) * BLOCK, :]
                h_ref[t, rows, at : at + 256] = piece
                square = piece * piece
                square = square[:, :LANES] + square[:, LANES:]
                squares[t] = square if n == 0 else squares[t] + square
        for t in range(FRAMES_IN):
            square_ref[b, t * BLOCK : (t + 1) * BLOCK, :] = squares[t]
        return carry

    lax.fori_loop(0, blocks, embed, 0)

    ones = jnp.ones((LANES, LANES), jnp.bfloat16)
    for layer in range(LAYERS):
        start = 2 * layer

        def scales(b, carry, start=start):
            mean = jnp.dot(
                square_ref[b, start * BLOCK :, :], ones, preferred_element_type=jnp.float32
            )
            scale = lax.rsqrt(mean * (1.0 / D) + 1e-06)
            for t in range(start, FRAMES_IN):
                piece = scale[(t - start) * BLOCK : (t - start + 1) * BLOCK, :]
                piece = jnp.where(frame0 + t >= 0, piece, 0.0)
                scale_ref[b, t * BLOCK : (t + 1) * BLOCK, :] = piece.astype(jnp.bfloat16)
            return carry

        lax.fori_loop(0, blocks, scales, 0)

        def convolve(b, carry, layer=layer, start=start):
            rows = pl.ds(pl.multiple_of(b * BLOCK, BLOCK), BLOCK)
            scale = [
                scale_ref[b, t * BLOCK : (t + 1) * BLOCK, :] for t in range(start, FRAMES_IN)
            ]

            def chunk(n, squares):
                squares = list(squares)
                for u in range(2):
                    cols = pl.ds(pl.multiple_of(n * 256 + u * LANES, LANES), LANES)
                    k0, k1, k2, shift = (coef_ref[layer, i, :, cols] for i in range(4))
                    two_back = h_ref[start, rows, cols] * scale[0]
                    one_back = h_ref[start + 1, rows, cols] * scale[1]
                    for t in range(start + 2, FRAMES_IN):
                        value = h_ref[t, rows, cols]
                        normed = value * scale[t - start]
                        half = (k0 * normed + k1 * one_back) + (k2 * two_back + shift)
                        value = value + (half + half * jnp.tanh(half))
                        h_ref[t, rows, cols] = value
                        if layer < LAYERS - 1:
                            squares[t - start - 2] = squares[t - start - 2] + value * value
                        two_back, one_back = one_back, normed
                return tuple(squares)

            zeros = jnp.zeros((BLOCK, LANES), jnp.bfloat16)
            squares = lax.fori_loop(0, D // 256, chunk, (zeros,) * (FRAMES_IN - start - 2))
            if layer < LAYERS - 1:
                for t in range(start + 2, FRAMES_IN):
                    square_ref[b, t * BLOCK : (t + 1) * BLOCK, :] = squares[t - start - 2]
            return carry

        lax.fori_loop(0, blocks, convolve, 0)

    def wipe(b, carry):
        rows = pl.ds(pl.multiple_of(b * BLOCK, BLOCK), BLOCK)
        for t in range(HALO, FRAMES_IN):
            h_ref[t, rows, :] = jnp.zeros((BLOCK, D), jnp.bfloat16)
        return carry

    lax.fori_loop(blocks, MAX_ROWS // BLOCK, wipe, 0)

    wide_row = lax.broadcasted_iota(jnp.int32, (MAX_ROWS, LANES), 1)
    spread = jnp.concatenate(
        [(place_ref[...] == wide_row + q * LANES).astype(jnp.bfloat16) for q in range(MAX_ROWS // LANES)],
        axis=1,
    )
    for t in range(F_DEV):

        def place(n, carry, t=t):
            cols = pl.ds(pl.multiple_of(n * 256, 256), 256)
            value = jnp.dot(spread, h_ref[HALO + t, :, cols], preferred_element_type=jnp.float32)
            staged_ref[t, :, cols] = value.astype(jnp.bfloat16)
            return carry

        lax.fori_loop(0, D // 256, place, 0)
        pltpu.make_async_copy(staged_ref.at[t], out_ref.at[t], sems.at[t]).start()
    for t in range(F_DEV):
        pltpu.make_async_copy(staged_ref.at[t], out_ref.at[t], sems.at[t]).wait()


def per_device(
    patches, owner_list, valid_rows, embed_weight, embed_bias, norm_gain, conv_kernel, conv_bias
):
    sources = lax.axis_size("space")
    chips = lax.axis_size("y")
    here = jnp.stack([lax.axis_index("y"), lax.axis_index("c"), lax.axis_index("space")])
    here = here.astype(jnp.int32)
    smem = pl.BlockSpec(memory_space=pltpu.SMEM)
    vmem = pl.BlockSpec(memory_space=pltpu.VMEM)
    width = TILE_ROWS * PF
    outgoing = pl.pallas_call(
        functools.partial(send_kernel, sources, chips * COPIED),
        out_shape=jax.ShapeDtypeStruct((chips * COPIED, width), jnp.bfloat16),
        in_specs=[smem, smem, vmem],
        out_specs=vmem,
        name="send",
    )(here[2:], owner_list, patches.reshape(F_DEV * TILES_DEV, width))
    arrived = lax.all_to_all(outgoing, ("y", "space"), split_axis=0, concat_axis=0, tiled=True)
    arrived = arrived.reshape(chips, COPIED, width)
    other = lax.ppermute(arrived, "c", [(0, 1), (1, 0)])
    core = lax.axis_index("c")
    got = jnp.stack([jnp.where(core == 0, arrived, other), jnp.where(core == 0, other, arrived)])
    packed = pl.pallas_call(
        functools.partial(main_kernel, sources),
        out_shape=jax.ShapeDtypeStruct((F_DEV, MAX_ROWS, D), jnp.bfloat16),
        in_specs=[smem, smem, smem] + [vmem] * 6,
        out_specs=pl.BlockSpec(memory_space=pl.ANY),
        scratch_shapes=[
            pltpu.SMEM((SLOTS_DEV + 1,), jnp.int32),
            pltpu.SMEM((SLOTS_DEV + 1,), jnp.int32),
            pltpu.VMEM((MAX_ROWS, LANES), jnp.int32),
            pltpu.VMEM((LAYERS, 4, BLOCK, D), jnp.bfloat16),
            pltpu.VMEM((2 * PF, D), jnp.bfloat16),
            pltpu.VMEM((FRAMES_IN * BLOCK, LANES), jnp.bfloat16),
            pltpu.VMEM((FRAMES_IN, MAX_ROWS, D), jnp.bfloat16),
            pltpu.VMEM((MAX_ROWS // BLOCK, FRAMES_IN * BLOCK, LANES), jnp.bfloat16),
            pltpu.VMEM((MAX_ROWS // BLOCK, FRAMES_IN * BLOCK, LANES), jnp.bfloat16),
            pltpu.VMEM((F_DEV, MAX_ROWS, D), jnp.bfloat16),
            pltpu.SemaphoreType.DMA((F_DEV,)),
        ],
        compiler_params=pltpu.CompilerParams(vmem_limit_bytes=48 << 20),
        name="layers",
    )(
        here,
        owner_list,
        valid_rows,
        got,
        embed_weight,
        embed_bias.reshape(1, D),
        norm_gain,
        conv_kernel.reshape(LAYERS * 3, D),
        conv_bias,
    )
    return packed.reshape(F_DEV, SLOTS_DEV, TILE_ROWS, D)


def solution(mesh):
    frames, space = mesh.shape["tm"], mesh.shape["space"]
    split = Mesh(mesh.devices.reshape(frames // 2, 2, space), ("y", "c", "space"))
    placed = (P(("y", "c"), "space", None), P(), P(), P(), P(), P(), P(), P())
    return jax.shard_map(
        per_device,
        mesh=split,
        in_specs=placed,
        out_specs=P(("y", "c"), "space", None, None),
        check_vma=False,
    )
```

time: 279 us -> 85.7 us (0.31); the launches traced: 275 us -> 85.3 us
  waiting for transfers between devices: 187 us -> 0.01 us
  Pallas kernels: 0 us -> 62.6 us
  other arithmetic: 44.7 us -> 0.17 us
  starting transfers between devices: 23.1 us -> 3.49 us
  blocking collectives: 0 us -> 13.3 us
  local copies, waits for them, and re-layouts: 17.5 us -> 5.69 us
    all_to_all x1 -> x0, waiting for transfers between devices: 120 us -> none  [per_device(): lax.all_to_all(outgoing, 'space', split_axis=1, concat_axis=1, tiled=True)]
    ppermute x4 -> x1, waiting for transfers between devices: 67 us -> 0.01 us  [per_device(): other = lax.ppermute(arrived, 'c', [(0, 1), (1, 0)])]
    pallas_call x0 -> x2, Pallas kernels: none -> 62.6 us  [the longest x1 60.8 us: per_device(): pl.pallas_call(functools.partial(main_kernel, sources), out_shape=jax.Sha...]
    convert_element_type x4 -> x0, other arithmetic: 17.4 us -> none  [per_device(): (framed[2:].astype(jnp.float32) + jax.nn.silu(mixed)).astype(jnp.bfloat16)]
    ppermute x4 -> x1, starting transfers between devices: 17.3 us -> 3.49 us  [per_device(): other = lax.ppermute(arrived, 'c', [(0, 1), (1, 0)])]
    all_to_all x0 -> x1, blocking collectives: none -> 13.3 us  [per_device(): lax.all_to_all(outgoing, ('y', 'space'), split_axis=0, concat_axis=0, til...]
    select_n x3 -> x0, other arithmetic: 9.47 us -> none  [the longest x2 6.16 us: per_device(): outgoing = jnp.take(hidden, chosen_tiles, axis=1)]
    mul x5 -> x0, other arithmetic: 8.86 us -> none  [the longest x4 8.86 us: rms_scale(): return values * lax.rsqrt(mean_square + 1e-06) * gain_row]
  transfers between devices with their start and end apart: 5 -> 1, of which waited for: 5 -> 0; matrix products, arithmetic and copies ran while one was open for 1% -> 1% of each run, Pallas kernels for 0% -> 0%
where the time goes in v1:
time: 85.7 us; the launch traced here: 85.3 us
  Pallas kernels  62.6 us (73%)
  blocking collectives  13.3 us (16%)
  local copies, waits for them, and re-layouts  5.69 us (7%)
  starting transfers between devices  3.49 us (4%)
    pallas_call x1, Pallas kernels, per_device(): pl.pallas_call(functools.partial(main_kernel, sources), out_shape=jax.Sha...  60.8 us
    all_to_all x1, blocking collectives, per_device(): lax.all_to_all(outgoing, ('y', 'space'), split_axis=0, concat_axis=0, til...  13.3 us
    unnamed x13, local copies, waits for them, and re-layouts  5.62 us
    ppermute x1, starting transfers between devices, per_device(): other = lax.ppermute(arrived, 'c', [(0, 1), (1, 0)])  3.49 us
    pallas_call x1, Pallas kernels, per_device(): pl.pallas_call(functools.partial(send_kernel, sources, chips * COPIED), o...  1.85 us
  transfers between devices with their start and end apart: 1, of which 0 were waited for; matrix products, arithmetic and copies ran while one was open for 1% of the time, Pallas kernels for 0%

profile of v1, /device:TPU:9, one launch (start us, length us, event | category | flops | bytes accessed | tf_op | source)
XLA Modules:
  0.0 85.3 jit_solution(5192356105152991792)
XLA Ops:
  0.0 1.9 %send.1 = bf16[256,512]{1,0:T(8,128)(2,1)} custom-call(s32[1]{0:T(128)} %bitcast.2.me_ref, s32[128]{0:T(128)} %owner_ref.3, bf16[64,512]{1,0:T(8,128)(2,1)} %bitcast.19), custom_call_target="tpu_custom_call" | custom-call | tf_op jit(solution)/shard_map/send/pallas_call | solution.py:246
  1.9 13.3 %all_to_all.9 = bf16[16,16,512]{2,1,0:T(8,128)(2,1)S(1)} all-to-all(bf16[16,16,512]{2,1,0:T(8,128)(2,1)} %bitcast.16), channel_id=1, replica_groups=mesh['y'=2,'c'=2,'space'=8] {'y','space'}, dimensions={0} | all-to-all | bytes 524288 | tf_op jit(solution)/shard_map/all_to_all | solution.py:253
  15.1 3.5 %collective-permute-start = (bf16[2,128,512]{2,1,0:T(8,128)(2,1)S(1)}, bf16[2,128,512]{2,1,0:T(8,128)(2,1)S(1)}, u32[]{:S(2)}, u32[]{:S(2)}) collective-permute-start(bf16[2,128,512]{2,1,0:T(8,128)(2,1)S(1)} %bitcast.17), channel_id=1, source_target_pairs={{0,8},{8,0},{1,9},{9,1},{2,10},{10,2},{3,11},{11,3},{4,12},{12,4},... | collective-permute-start | bytes 786440 | tf_op jit(solution)/shard_map/ppermute | solution.py:255
  18.6 1.0 %copy.10 = f32[4,3,3072]{2,1,0:T(4,128)S(1)} copy(f32[4,3,3072]{2,0,1:T(4,128)} %param.14) | data formatting | bytes 294912 | tf_op args[6]
  19.6 0.1 reshape.21.conv_ref
  19.7 0.1 pad_add_fusion.at_ref
  19.8 0.0 collective-permute-done
  19.8 0.1 pad_maximum_fusion.got_ref
  19.9 0.0 copy-start
  19.9 1.0 %copy-done = bf16[64,3072]{1,0:T(8,128)(2,1)S(1)} copy-done((bf16[64,3072]{1,0:T(8,128)(2,1)S(1)}, bf16[64,3072]{1,0:T(8,128)(2,1)}, u32[]{:S(2)}) %copy-start) | copy-done | bytes 393240
  20.9 0.0 copy-start.1
  20.9 0.8 copy-done.1
  21.7 0.0 copy-start.2
  21.7 0.8 copy-done.2
  22.5 0.0 copy-start.3
  22.5 0.7 copy-done.3
  23.2 0.0 copy-start.4
  23.2 0.7 copy-done.4
  23.9 0.0 copy-start.5
  23.9 0.7 copy-done.5
  24.5 60.8 %layers.1 = bf16[4,256,3072]{2,1,0:T(8,128)(2,1)} custom-call(s32[3]{0:T(128)S(1)} %pad_add_fusion.at_ref, s32[128]{0:T(128)S(1)} %copy-done.4, s32[128]{0:T(128)S(1)} %copy-done.5, bf16[2,2,128,512]{3,2,1,0:T(8,128)(2,1)S(1)} %pad_maximum_fusion.got_ref, bf16[64,3072]{1,0:T(8,128)(2,1)S(1)} %copy-done, f32[1,3072]{1,0:T(1,128)S(1)} %bitcast.15, ...), custom_call_target="tpu_custom_call" | custom-call | tf_op jit(solution)/shard_map/layers/pallas_call | solution.py:258
  (1 shorter events, 0.0 us)
Async XLA Ops:
  15.1 4.7 %collective-permute-start = (bf16[2,128,512]{2,1,0:T(8,128)(2,1)S(1)}, bf16[2,128,512]{2,1,0:T(8,128)(2,1)S(1)}, u32[]{:S(2)}, u32[]{:S(2)}) collective-permute-start(bf16[2,128,512]{2,1,0:T(8,128)(2,1)S(1)} %bitcast.17), channel_id=1, source_target_pairs={{0,8},{8,0},{1,9},{9,1},{2,10},{10,2},{3,11},{11,3},{4,12},{12,4},... | collective-permute-start | bytes 786440 | tf_op jit(solution)/shard_map/ppermute | solution.py:255
  19.9 1.0 %copy-start = (bf16[64,3072]{1,0:T(8,128)(2,1)S(1)}, bf16[64,3072]{1,0:T(8,128)(2,1)}, u32[]{:S(2)}) copy-start(bf16[64,3072]{1,0:T(8,128)(2,1)} %weight_ref.1) | copy-start | bytes 1179652
  20.9 0.8 copy-start.1
  21.7 0.8 copy-start.2
  22.5 0.7 copy-start.3
  23.2 0.7 copy-start.4
  23.9 0.7 copy-start.5
